TPU v7x, 32 devices: a whole 2x2x4 slice. The times are simulated.
32 devices in a mesh: seq: 4 (over z), batch: 4 (over x, core), tensor: 2 (over y).
Axes of the slice: x: 2, y: 2, z: 4, core: 2. Of those that a mesh axis runs over, the one named last changes fastest.
Arguments:
- inputs: bfloat16 [4, 1024, 768], P('batch', 'seq'), may hold values from -16 to 16
- history: bfloat16 [8, 4, 1024, 768], P(None, 'batch', 'seq'), may hold values from -6 to 6
- window_lengths: int32 [4, 3], P('batch'), may hold values from 1 to 768, 1024 in all within a row
- block_order: int32 [4], replicated, may hold values from 0 to 3, each once
- first_gain: float32 [768], replicated, may hold values from 0.5 to 1.5
- first_shift: float32 [768], replicated, may hold values from -1.5 to 1.5
- query_weight: bfloat16 [768, 768], P(None, 'tensor'), may hold values from -0.21875 to 0.21875
- key_weight: bfloat16 [768, 768], P(None, 'tensor'), may hold values from -0.21875 to 0.21875
- value_weight: bfloat16 [768, 768], P(None, 'tensor'), may hold values from -0.21875 to 0.21875
- out_weight: bfloat16 [768, 768], P('tensor'), may hold values from -1.75 to 1.75
- second_gain: float32 [768], replicated, may hold values from 0.5 to 1.5
- second_shift: float32 [768], replicated, may hold values from -1.5 to 1.5
- up_weight: bfloat16 [768, 3072], P(None, 'tensor'), may hold values from -0.21875 to 0.21875
- up_bias: float32 [3072], P('tensor'), may hold values from -2.5 to 2.5
- down_weight: bfloat16 [3072, 768], P('tensor'), may hold values from -0.109375 to 0.109375
- down_bias: float32 [768], replicated, may hold values from -1.5 to 1.5
- mix_weights: float32 [9], replicated, may hold values from -2.5 to 2.5
- cotangent_next: bfloat16 [4, 1024, 768], P('batch', 'seq'), may hold values from -6 to 6
- cotangent_block: bfloat16 [4, 1024, 768], P('batch', 'seq'), may hold values from -6 to 6
Outputs:
- next_input: bfloat16 [4, 1024, 768], P('batch', 'seq')
- block_output: bfloat16 [4, 1024, 768], P('batch', 'seq')
- grad_input: bfloat16 [4, 1024, 768], P('batch', 'seq')
- grad_history: bfloat16 [8, 4, 1024, 768], P(None, 'batch', 'seq')
- grad_first_gain: float32 [768], replicated
- grad_first_shift: float32 [768], replicated
- grad_query_weight: float32 [768, 768], P(('seq', 'batch'), 'tensor')
- grad_key_weight: float32 [768, 768], P(('seq', 'batch'), 'tensor')
- grad_value_weight: float32 [768, 768], P(('seq', 'batch'), 'tensor')
- grad_out_weight: float32 [768, 768], P('tensor', ('seq', 'batch'))
- grad_second_gain: float32 [768], replicated
- grad_second_shift: float32 [768], replicated
- grad_up_weight: float32 [768, 3072], P(('seq', 'batch'), 'tensor')
- grad_up_bias: float32 [3072], P('tensor')
- grad_down_weight: float32 [3072, 768], P('tensor', ('seq', 'batch'))
- grad_down_bias: float32 [768], replicated
- grad_mix_weights: float32 [9], replicated
- rms_values: float32 [3], replicated
Inputs may be any that keep to these rules, and one draw needn't show every extreme that they name: `window_lengths`: each row sums to 1024; the longest window of each row has exactly 768 tokens. A permutation; index i of seq holds positions block_order[i] * 256 to block_order[i] * 256 + 255 of each sequence.
All inputs are finite; a program needn't handle non-finite values.
Results may differ from a plain program's by a relative error of at most 0.025.
Values may be sent and summed in bfloat16 or wider, within the bound.
A program may use at most 192 MiB of HBM per device.

v0:
```python
import jax
import jax.numpy as jnp
from jax import lax
from jax.sharding import PartitionSpec as P

HEAD_DIM = 64
epsilon = 1e-05


def layer_parts(values, gain, shift):
    centre = jnp.mean(values, axis=-1, keepdims=True)
    centred = values - centre
    spread = jnp.mean(centred * centred, axis=-1, keepdims=True)
    inverse = lax.rsqrt(spread + epsilon)
    unit = centred * inverse
    return (unit * gain + shift, unit, inverse)


def norm_backward(grad_out, unit, inverse, gain):
    scaled = grad_out * gain
    return inverse * (
        scaled
        - jnp.mean(scaled, axis=-1, keepdims=True)
        - unit * jnp.mean(scaled * unit, axis=-1, keepdims=True)
    )


def gelu_tanh(values):
    return (
        0.5
        * values
        * (1.0 + jnp.tanh(0.7978845608028654 * (values + 0.044715 * values * values * values)))
    )


def rotate(values, cosine, sine):
    half = values.shape[-1] // 2
    first = values[..., :half]
    second = values[..., half:]
    return jnp.concatenate(
        [first * cosine - second * sine, second * cosine + first * sine], axis=-1
    )


def keep_state(state):
    return state


def per_device(
    inputs,
    history,
    window_lengths,
    block_order,
    first_gain,
    first_shift,
    query_weight,
    key_weight,
    value_weight,
    out_weight,
    second_gain,
    second_shift,
    up_weight,
    up_bias,
    down_weight,
    down_bias,
    mix_weights,
    cotangent_next,
    cotangent_block,
):
    rows = inputs.shape[1]
    width = inputs.shape[2]
    local_width = query_weight.shape[1]
    heads = local_width // HEAD_DIM
    half = HEAD_DIM // 2
    depth = history.shape[0]
    total = rows * lax.axis_size("seq")
    size = min(1024, total)
    count = total // size
    split = (rows, heads, HEAD_DIM)
    offsets = jnp.arange(rows, dtype=jnp.int32)
    own_pos = block_order[lax.axis_index("seq")] * rows + offsets
    every_row = jnp.arange(total, dtype=jnp.int32)
    every_pos = block_order[every_row // rows] * rows + every_row % rows
    ends = jnp.cumsum(window_lengths[0])
    own_docs = jnp.sum((own_pos[:, None] >= ends[None, :]).astype(jnp.int32), axis=1)
    every_docs = jnp.sum((every_pos[:, None] >= ends[None, :]).astype(jnp.int32), axis=1)
    rates = jnp.exp(-jnp.log(10000.0) * jnp.arange(half, dtype=jnp.float32) / half)
    angles = own_pos.astype(jnp.float32)[:, None] * rates[None, :]
    cosine = jnp.cos(angles)[:, None, :]
    sine = jnp.sin(angles)[:, None, :]
    residual = inputs[0].astype(jnp.float32)
    normed_first, unit_first, scale_first = layer_parts(residual, first_gain, first_shift)
    normed_first = normed_first.astype(jnp.bfloat16)
    query_lin = jnp.dot(normed_first, query_weight, preferred_element_type=jnp.float32)
    key_lin = jnp.dot(normed_first, key_weight, preferred_element_type=jnp.float32)
    value_lin = jnp.dot(normed_first, value_weight, preferred_element_type=jnp.float32)
    queries = (rotate(query_lin.reshape(split), cosine, sine) * 0.125).astype(jnp.bfloat16)
    keys = (
        rotate(key_lin.reshape(split), cosine, sine).reshape(rows, local_width).astype(jnp.bfloat16)
    )
    values = value_lin.astype(jnp.bfloat16)
    all_keys, all_values = (
        lax.all_gather(keys, "seq", axis=0, tiled=True),
        lax.all_gather(values, "seq", axis=0, tiled=True),
    )

    def block_mask(index):
        key_pos = lax.dynamic_slice_in_dim(every_pos, index * size, size)
        key_docs = lax.dynamic_slice_in_dim(every_docs, index * size, size)
        return (key_pos[None, :] <= own_pos[:, None]) & (key_docs[None, :] == own_docs[:, None])

    def block_rows(array, index):
        return lax.dynamic_slice_in_dim(array, index * size, size).reshape(size, heads, HEAD_DIM)

    def block_scores(index, key_rows):
        return jnp.einsum(
            "qhd,khd->hqk", queries, block_rows(key_rows, index), preferred_element_type=jnp.float32
        )

    def stats_step(index, carry):
        allowed = block_mask(index)

        def update(state):
            peak, denom = state
            masked = jnp.where(allowed[None], block_scores(index, all_keys), -1e30)
            fresh = jnp.maximum(peak, jnp.max(masked, axis=-1))
            weights = jnp.where(allowed[None], jnp.exp(masked - fresh[..., None]), 0.0)
            return (fresh, denom * jnp.exp(peak - fresh) + jnp.sum(weights, axis=-1))

        return lax.cond(jnp.any(allowed), update, keep_state, carry)

    start_stats = (
        jnp.full((heads, rows), -1e30, jnp.float32),
        jnp.zeros((heads, rows), jnp.float32),
    )
    peak, denom = lax.fori_loop(0, count, stats_step, start_stats)

    def block_probs(index, allowed, key_rows):
        scores = block_scores(index, key_rows)
        return jnp.where(allowed[None], jnp.exp(scores - peak[..., None]), 0.0) / denom[..., None]

    def output_step(index, carry):
        allowed = block_mask(index)

        def output_accumulate(state):
            probs_low = block_probs(index, allowed, all_keys).astype(jnp.bfloat16)
            return state + jnp.einsum(
                "hqk,khd->qhd",
                probs_low,
                block_rows(all_values, index),
                preferred_element_type=jnp.float32,
            )

        return lax.cond(jnp.any(allowed), output_accumulate, keep_state, carry)

    running = lax.fori_loop(0, count, output_step, jnp.zeros(split, jnp.float32))
    mixed = running.reshape(rows, local_width).astype(jnp.bfloat16)
    attn_out = lax.psum(
        jnp.dot(mixed, out_weight, preferred_element_type=jnp.float32).astype(jnp.bfloat16),
        "tensor",
    ).astype(jnp.float32)
    hidden = residual + attn_out
    normed_second, unit_second, scale_second = layer_parts(hidden, second_gain, second_shift)
    normed_second = normed_second.astype(jnp.bfloat16)
    upward = jnp.dot(normed_second, up_weight, preferred_element_type=jnp.float32) + up_bias
    active_full, gelu_pull = jax.vjp(gelu_tanh, upward)
    active = active_full.astype(jnp.bfloat16)
    mlp_out = (
        lax.psum(
            jnp.dot(active, down_weight, preferred_element_type=jnp.float32).astype(jnp.bfloat16),
            "tensor",
        ).astype(jnp.float32)
        + down_bias
    )
    block_value = hidden + mlp_out
    history_low = history[:, 0]
    next_value = (
        jnp.sum(mix_weights[:depth, None, None] * history_low.astype(jnp.float32), axis=0)
        + mix_weights[depth] * block_value
    )
    cot_low = cotangent_next[0]
    cot_next = cot_low.astype(jnp.float32)
    cot_block = cotangent_block[0].astype(jnp.float32)
    grad_history = (mix_weights[:depth, None, None] * cot_next[None]).astype(jnp.bfloat16)
    mix_terms = jnp.concatenate(
        [
            jnp.einsum("jsd,sd->j", history_low, cot_low, preferred_element_type=jnp.float32),
            jnp.sum(block_value * cot_next)[None],
        ]
    )
    grad_block = cot_block + mix_weights[depth] * cot_next
    grad_mlp = grad_block.astype(jnp.bfloat16)
    grad_down = jnp.einsum("sf,sd->fd", active, grad_mlp, preferred_element_type=jnp.float32)
    grad_active = jnp.einsum("sd,fd->sf", grad_mlp, down_weight, preferred_element_type=jnp.float32)
    grad_up = gelu_pull(grad_active)[0].astype(jnp.bfloat16)
    grad_upw = jnp.einsum("sd,sf->df", normed_second, grad_up, preferred_element_type=jnp.float32)
    grad_normed_second = lax.psum(
        jnp.einsum("sf,df->sd", grad_up, up_weight, preferred_element_type=jnp.float32).astype(
            jnp.bfloat16
        ),
        "tensor",
    ).astype(jnp.float32)
    grad_hidden = grad_block + norm_backward(
        grad_normed_second, unit_second, scale_second, second_gain
    )
    grad_attn = grad_hidden.astype(jnp.bfloat16)
    grad_outw = jnp.einsum("sk,sd->kd", mixed, grad_attn, preferred_element_type=jnp.float32)
    grad_mixed = (
        jnp.einsum("sd,kd->sk", grad_attn, out_weight, preferred_element_type=jnp.float32)
        .astype(jnp.bfloat16)
        .reshape(split)
    )
    back_keys, back_values = (
        lax.all_gather(keys, "seq", axis=0, tiled=True),
        lax.all_gather(values, "seq", axis=0, tiled=True),
    )

    def delta_step(index, carry):
        allowed = block_mask(index)

        def delta_accumulate(state):
            probs = block_probs(index, allowed, back_keys)
            grad_probs = jnp.einsum(
                "qhd,khd->hqk",
                grad_mixed,
                block_rows(back_values, index),
                preferred_element_type=jnp.float32,
            )
            return state + jnp.sum(probs * grad_probs, axis=-1)

        return lax.cond(jnp.any(allowed), delta_accumulate, keep_state, carry)

    delta = lax.fori_loop(0, count, delta_step, jnp.zeros((heads, rows), jnp.float32))

    def grad_step(index, carry):
        allowed = block_mask(index)

        def grad_accumulate(state):
            grad_queries, key_buffer, value_buffer = state
            key_rows = block_rows(back_keys, index)
            value_rows = block_rows(back_values, index)
            probs = block_probs(index, allowed, back_keys)
            grad_probs = jnp.einsum(
                "qhd,khd->hqk", grad_mixed, value_rows, preferred_element_type=jnp.float32
            )
            grad_scores = (probs * (grad_probs - delta[..., None])).astype(jnp.bfloat16)
            grad_queries = grad_queries + jnp.einsum(
                "hqk,khd->qhd", grad_scores, key_rows, preferred_element_type=jnp.float32
            )
            key_part = jnp.einsum(
                "hqk,qhd->khd", grad_scores, queries, preferred_element_type=jnp.float32
            ).reshape(size, local_width)
            value_part = jnp.einsum(
                "hqk,qhd->khd",
                probs.astype(jnp.bfloat16),
                grad_mixed,
                preferred_element_type=jnp.float32,
            ).reshape(size, local_width)
            key_buffer = lax.dynamic_update_slice_in_dim(key_buffer, key_part, index * size, 0)
            value_buffer = lax.dynamic_update_slice_in_dim(
                value_buffer, value_part, index * size, 0
            )
            return (grad_queries, key_buffer, value_buffer)

        return lax.cond(jnp.any(allowed), grad_accumulate, keep_state, carry)

    start_grads = (
        jnp.zeros(split, jnp.float32),
        jnp.zeros((total, local_width), jnp.float32),
        jnp.zeros((total, local_width), jnp.float32),
    )
    grad_queries, key_buffer, value_buffer = lax.fori_loop(0, count, grad_step, start_grads)
    grad_keys, grad_values = (
        lax.psum_scatter(
            key_buffer.astype(jnp.bfloat16), "seq", scatter_dimension=0, tiled=True
        ).astype(jnp.float32),
        lax.psum_scatter(
            value_buffer.astype(jnp.bfloat16), "seq", scatter_dimension=0, tiled=True
        ).astype(jnp.float32),
    )
    grad_query_lin = (
        rotate(grad_queries * 0.125, cosine, -sine).reshape(rows, local_width).astype(jnp.bfloat16)
    )
    grad_key_lin = (
        rotate(grad_keys.reshape(split), cosine, -sine)
        .reshape(rows, local_width)
        .astype(jnp.bfloat16)
    )
    grad_value_lin = grad_values.astype(jnp.bfloat16)
    grad_queryw = jnp.einsum(
        "sd,se->de", normed_first, grad_query_lin, preferred_element_type=jnp.float32
    )
    grad_keyw = jnp.einsum(
        "sd,se->de", normed_first, grad_key_lin, preferred_element_type=jnp.float32
    )
    grad_valuew = jnp.einsum(
        "sd,se->de", normed_first, grad_value_lin, preferred_element_type=jnp.float32
    )
    local_normed = jnp.einsum(
        "se,de->sd", grad_query_lin, query_weight, preferred_element_type=jnp.float32
    )
    local_normed = local_normed + jnp.einsum(
        "se,de->sd", grad_key_lin, key_weight, preferred_element_type=jnp.float32
    )
    local_normed = local_normed + jnp.einsum(
        "se,de->sd", grad_value_lin, value_weight, preferred_element_type=jnp.float32
    )
    grad_normed_first = lax.psum(local_normed.astype(jnp.bfloat16), "tensor").astype(jnp.float32)
    grad_input = grad_hidden + norm_backward(grad_normed_first, unit_first, scale_first, first_gain)
    shared_grads = (
        lax.psum_scatter(grad_queryw, ("seq", "batch"), scatter_dimension=0, tiled=True),
        lax.psum_scatter(grad_keyw, ("seq", "batch"), scatter_dimension=0, tiled=True),
        lax.psum_scatter(grad_valuew, ("seq", "batch"), scatter_dimension=0, tiled=True),
        lax.psum_scatter(grad_outw, ("seq", "batch"), scatter_dimension=1, tiled=True),
        lax.psum_scatter(grad_upw, ("seq", "batch"), scatter_dimension=0, tiled=True),
        lax.psum_scatter(grad_down, ("seq", "batch"), scatter_dimension=1, tiled=True),
    )
    square_terms = jnp.stack(
        [
            jnp.sum(block_value * block_value),
            jnp.sum(attn_out * attn_out),
            jnp.sum(mlp_out * mlp_out),
        ]
    )
    small_terms = lax.psum(
        (
            jnp.sum(grad_normed_first * unit_first, axis=0),
            jnp.sum(grad_normed_first, axis=0),
            jnp.sum(grad_normed_second * unit_second, axis=0),
            jnp.sum(grad_normed_second, axis=0),
            jnp.sum(grad_up.astype(jnp.float32), axis=0),
            jnp.sum(grad_mlp.astype(jnp.float32), axis=0),
            mix_terms,
            square_terms,
        ),
        ("seq", "batch"),
    )
    entries = float(lax.axis_size("batch") * total * width)
    rms_values = jnp.sqrt(small_terms[7] / entries)
    return (
        next_value.astype(jnp.bfloat16)[None],
        block_value.astype(jnp.bfloat16)[None],
        grad_input.astype(jnp.bfloat16)[None],
        grad_history[:, None],
        small_terms[0],
        small_terms[1],
        shared_grads[0],
        shared_grads[1],
        shared_grads[2],
        shared_grads[3],
        small_terms[2],
        small_terms[3],
        shared_grads[4],
        small_terms[4],
        shared_grads[5],
        small_terms[5],
        small_terms[6],
        rms_values,
    )


def solution(mesh):
    in_specs = (
        P("batch", "seq", None),
        P(None, "batch", "seq", None),
        P("batch", None),
        P(),
        P(),
        P(),
        P(None, "tensor"),
        P(None, "tensor"),
        P(None, "tensor"),
        P("tensor", None),
        P(),
        P(),
        P(None, "tensor"),
        P("tensor"),
        P("tensor", None),
        P(),
        P(),
        P("batch", "seq", None),
        P("batch", "seq", None),
    )
    out_specs = (
        P("batch", "seq", None),
        P("batch", "seq", None),
        P("batch", "seq", None),
        P(None, "batch", "seq", None),
        P(),
        P(),
        P(("seq", "batch"), "tensor"),
        P(("seq", "batch"), "tensor"),
        P(("seq", "batch"), "tensor"),
        P("tensor", ("seq", "batch")),
        P(),
        P(),
        P(("seq", "batch"), "tensor"),
        P("tensor"),
        P("tensor", ("seq", "batch")),
        P(),
        P(),
        P(),
    )
    return jax.shard_map(
        per_device, mesh=mesh, in_specs=in_specs, out_specs=out_specs, check_vma=False
    )
```

profile of v0, /device:TPU:0, one launch (start us, length us, event | category | flops | bytes accessed | tf_op | source)
XLA Modules:
  0.0 684.2 jit_solution(1408262053932993367)
XLA Ops:
  9.9 2.1 copy.54
  13.2 2.3 fusion.53
  15.4 2.4 fusion.55
  19.9 2.1 multiply_subtract_fusion.2
  22.0 21.7 %all_gather.8 = bf16[1024,384]{0,1:T(8,128)(2,1)} all-gather(bf16[256,384]{0,1:T(8,128)(2,1)S(1)} %bitcast.211), channel_id=1, replica_groups=mesh['seq'=4,'batch'=4,'tensor'=2] {'seq'}, dimensions={0}, use_global_device_ids=true | all-gather | bytes 983040 | tf_op jit(solution)/shard_map/all_gather | solution.py:103
  43.7 2.6 fusion.67
  46.7 1.6 fusion.82
  49.5 17.3 %all_gather.9 = bf16[1024,384]{1,0:T(8,128)(2,1)S(1)} all-gather(bf16[256,384]{1,0:T(8,128)(2,1)S(1)} %convolution_convert_fusion.4), channel_id=1, replica_groups=mesh['seq'=4,'batch'=4,'tensor'=2] {'seq'}, dimensions={0}, use_global_device_ids=true | all-gather | bytes 983040 | tf_op jit(solution)/shard_map/all_gather | solution.py:104
  68.1 6.7 conditional.4
  68.1 2.1 select_reduce_fusion.1
  71.0 1.9 select_reduce_fusion
  75.6 6.0 conditional.5
  76.7 4.8 fusion.4
  83.3 2.2 convolution_convert_fusion.2
  87.0 3.2 convert_reduce_fusion.4
  90.3 21.2 %all-reduce.6.cloned.1.call-done = bf16[256,768]{1,0:T(8,128)(2,1)} async-done(((bf16[256,768]{1,0:T(8,128)(2,1)}), bf16[256,768]{1,0:T(8,128)(2,1)}) %all-reduce.6.cloned.1.call-update) | async-done | bytes 393232 | tf_op jit(solution)/shard_map/psum | solution.py:158
  114.5 2.7 convolution_add_fusion
  117.3 1.8 convolution_convert_fusion.1
  119.1 2.4 convert_reduce_fusion
  124.0 2.8 multiply_reduce_fusion.2
  126.8 31.8 %all-reduce.10.cloned.1.call-done = (bf16[256,768]{1,0:T(8,128)(2,1)}, bf16[256,768]{1,0:T(8,128)(2,1)}) async-done(((bf16[256,768]{1,0:T(8,128)(2,1)}, bf16[256,768]{1,0:T(8,128)(2,1)}), (bf16[256,768]{1,0:T(8,128)(2,1)}, bf16[256,768]{1,0:T(8,128)(2,1)})) %all-reduce.10.cloned.1.call-update) | async-done | bytes 786448 | tf_op jit(solution)/shard_map/psum | solution.py:169
  158.7 4.3 multiply_reduce_fusion.4
  165.3 1.8 copy.56
  167.0 11.1 %conditional.6 = (f32[6,256]{1,0:T(8,128)S(1)}) conditional(s32[]{:T(128)} %convert_element_type.198, f32[6,256]{1,0:T(8,128)S(1)} %broadcast.362, (pred[256,1024]{1,0:T(8,128)(4,1)}, bf16[1024,384]{0,1:T(8,128)(2,1)S(1)}, bf16[256,6,64]{0,2,1:T(8,128)(2,1)}, f32[6,256]{1,0:T(8,128)}, f32[6,256]{1,0:T(8,128)}, ...), branch_computations={%region_20.21_spmd, %region_21.23_spmd} | conditional | flops 410517504 | bytes 16420872 | solution.py:231
  167.0 4.6 fusion.84
  172.8 5.3 multiply_reduce_fusion
  178.1 17.4 %conditional.7 = (f32[256,6,64]{0,2,1:T(8,128)}, bf16[1024,384]{0,1:T(8,128)(2,1)}, bf16[1024,384]{0,1:T(8,128)(2,1)S(1)}) conditional(s32[]{:T(128)} %convert_element_type.198, f32[256,6,64]{0,2,1:T(8,128)} %broadcast.358, (pred[256,1024]{1,0:T(8,128)(4,1)}, bf16[1024,384]{0,1:T(8,128)(2,1)S(1)}, bf16[256,6,64]{0,2,1:T(8,128)(2,1)}, ...), branch_computations={%region_23.24_spmd, %region_24.25_spmd} | conditional | flops 1017741312 | bytes 61622352 | solution.py:265
  178.4 5.5 select_divide_fusion
  185.1 4.2 multiply_convert_fusion
  189.3 2.6 fusion.85
  191.9 2.9 fusion.8
  197.5 21.5 %reduce-scatter.9.cloned.1.call-done = bf16[256,384]{0,1:T(8,128)(2,1)} async-done(((bf16[1024,384]{0,1:T(8,128)(2,1)}), bf16[256,384]{0,1:T(8,128)(2,1)}) %reduce-scatter.9.cloned.1.call-update) | async-done | bytes 196624 | tf_op jit(solution)/shard_map/reduce_scatter | solution.py:274
  222.4 21.4 %reduce-scatter.11.cloned.1.call-done = bf16[256,384]{0,1:T(8,128)(2,1)} async-done(((bf16[1024,384]{0,1:T(8,128)(2,1)}), bf16[256,384]{0,1:T(8,128)(2,1)}) %reduce-scatter.11.cloned.1.call-update) | async-done | bytes 196624 | tf_op jit(solution)/shard_map/reduce_scatter | solution.py:277
  243.8 2.3 fusion.15
  251.1 1.6 fusion.72
  252.9 3.1 fusion.64
  257.4 3.1 fusion.75
  261.2 2.5 multiply_convert_fusion.1
  266.0 2.4 pad_maximum_fusion.2
  268.4 3.1 all-reduce.8.cloned.1.call-done
  271.5 2.0 fusion.46
  273.5 62.1 %all-reduce = (f32[768]{0:T(1024)}, f32[768]{0:T(1024)}, f32[768]{0:T(1024)}, f32[768]{0:T(1024)}, f32[1536]{0:T(1024)}, /*index=5*/f32[768]{0:T(1024)}, f32[9]{0:T(128)}, f32[3]{0:T(128)}) all-reduce(f32[768]{0:T(1024)} %get-tuple-element.439, ...), channel_id=1, replica_groups=mesh['seq'=4,'batch'=4,'tensor'=2] {'seq','batch'}, use_global_device_ids=true, to_apply=%region_31.32 | all-reduce | flops 5388 | bytes 43104 | tf_op jit(solution)/shard_map/psum | solution.py:325
  338.1 2.1 fusion.51
  340.1 55.5 %reduce-scatter.15.cloned.1.call-done = f32[48,384]{1,0:T(8,128)} async-done(((f32[768,384]{1,0:T(8,128)}), f32[48,384]{1,0:T(8,128)}) %reduce-scatter.15.cloned.1.call-update) | async-done | bytes 73744 | tf_op jit(solution)/shard_map/reduce_scatter | solution.py:312
  395.6 61.9 %reduce-scatter.13.cloned.1.call-done = f32[48,384]{1,0:T(8,128)} async-done(((f32[768,384]{1,0:T(8,128)}), f32[48,384]{1,0:T(8,128)}) %reduce-scatter.13.cloned.1.call-update) | async-done | bytes 73744 | tf_op jit(solution)/shard_map/reduce_scatter | solution.py:311
  457.5 61.7 %reduce-scatter.17.cloned.1.call-done = f32[48,384]{1,0:T(8,128)} async-done(((f32[768,384]{1,0:T(8,128)}), f32[48,384]{1,0:T(8,128)}) %reduce-scatter.17.cloned.1.call-update) | async-done | bytes 73744 | tf_op jit(solution)/shard_map/reduce_scatter | solution.py:313
  519.2 79.4 %reduce-scatter.21.cloned.1.call-done = f32[48,1536]{1,0:T(8,128)} async-done(((f32[768,1536]{1,0:T(8,128)}), f32[48,1536]{1,0:T(8,128)}) %reduce-scatter.21.cloned.1.call-update) | async-done | bytes 294928 | tf_op jit(solution)/shard_map/reduce_scatter | solution.py:315
  598.6 79.1 %reduce-scatter.23.cloned.1.call-done = f32[1536,48]{0,1:T(8,128)} async-done(((f32[1536,768]{0,1:T(8,128)}), f32[1536,48]{0,1:T(8,128)}) %reduce-scatter.23.cloned.1.call-update) | async-done | bytes 294928 | tf_op jit(solution)/shard_map/reduce_scatter | solution.py:316
  (203 shorter events, 42.9 us)
Async XLA Ops:
  7.2 110.0 %copy-start = (bf16[1536,768]{1,0:T(8,128)(2,1)S(1)}, bf16[1536,768]{1,0:T(8,128)(2,1)}, u32[]{:S(2)}) copy-start(bf16[1536,768]{1,0:T(8,128)(2,1)} %param.41) | copy-start | bytes 7077892
  7.2 5.9 copy-start.2
  7.2 4.8 copy-start.17
  7.2 5.9 copy-start.39
  7.2 5.9 copy-start.43
  7.3 104.2 %all-reduce.6.cloned.1.call-start = ((), (), s32[]{:S(2)}) async-start(), calls=%async_computation.8 | async-start | bytes 786432 | tf_op jit(solution)/shard_map/psum | solution.py:158
  8.7 40.3 %copy-start.41 = (f32[256]{0:T(256)}, f32[256]{0:T(256)S(1)}, u32[]{:S(2)}) copy-start(f32[256]{0:T(256)S(1)} %broadcast_multiply_fusion.6) | copy-start | bytes 3076
  9.9 39.0 %copy-start.45 = (f32[256]{0:T(256)}, f32[256]{0:T(256)S(1)}, u32[]{:S(2)}) copy-start(f32[256]{0:T(256)S(1)} %add_rsqrt_fusion.1) | copy-start | bytes 3076
  12.1 5.7 copy-start.57
  15.4 30.9 %copy-start.62 = (s32[1,3]{1,0:T(1,128)S(1)}, s32[1,3]{1,0:T(1,128)}, u32[]{:S(2)}) copy-start(s32[1,3]{1,0:T(1,128)} %param.29) | copy-start | bytes 40
  15.4 33.5 %copy-start.34 = (bf16[768,384]{1,0:T(8,128)(2,1)S(1)}, bf16[768,384]{1,0:T(8,128)(2,1)}, u32[]{:S(2)}) copy-start(bf16[768,384]{1,0:T(8,128)(2,1)} %param.35) | copy-start | bytes 1769476
  19.9 23.8 %copy-start.35 = (f32[256,32]{0,1:T(8,128)}, f32[256,32]{0,1:T(8,128)S(1)}, u32[]{:S(2)}) copy-start(f32[256,32]{0,1:T(8,128)S(1)} %get-tuple-element.485) | copy-start | bytes 98308
  49.0 17.8 %copy-start.31 = (f32[256,6,32]{0,2,1:T(8,128)S(1)}, f32[256,6,32]{0,2,1:T(8,128)}, u32[]{:S(2)}) copy-start(f32[256,6,32]{0,2,1:T(8,128)} %get-tuple-element.473) | copy-start | bytes 589828
  49.0 17.8 %copy-start.32 = (f32[256,6,32]{0,2,1:T(8,128)S(1)}, f32[256,6,32]{0,2,1:T(8,128)}, u32[]{:S(2)}) copy-start(f32[256,6,32]{0,2,1:T(8,128)} %get-tuple-element.474) | copy-start | bytes 589828
  49.0 19.1 %copy-start.8 = (bf16[1024,384]{0,1:T(8,128)(2,1)S(1)}, bf16[1024,384]{0,1:T(8,128)(2,1)}, u32[]{:S(2)}) copy-start(bf16[1024,384]{0,1:T(8,128)(2,1)} %all_gather.8) | copy-start | bytes 2359300
  49.0 19.1 %copy-start.16 = (pred[256,1024]{1,0:T(8,128)(4,1)S(1)}, pred[256,1024]{1,0:T(8,128)(4,1)}, u32[]{:S(2)}) copy-start(pred[256,1024]{1,0:T(8,128)(4,1)} %get-tuple-element.464) | copy-start | bytes 786436
  81.6 32.9 %copy-start.37 = (f32[768]{0:T(1024)S(1)}, f32[768]{0:T(1024)}, u32[]{:S(2)}) copy-start(f32[768]{0:T(1024)} %param.37) | copy-start | bytes 9220
  85.5 73.1 %all-reduce.10.cloned.1.call-start = ((), (), s32[]{:S(2)}) async-start(), calls=%async_computation.18 | async-start | bytes 1572864 | tf_op jit(solution)/shard_map/psum | solution.py:169
  123.9 34.7 %copy-start.4 = (bf16[256,768]{1,0:T(8,128)(2,1)S(1)}, bf16[256,768]{1,0:T(8,128)(2,1)}, u32[]{:S(2)}) copy-start(bf16[256,768]{1,0:T(8,128)(2,1)} %all-reduce.6.cloned.1.call-done) | copy-start | bytes 1179652
  123.9 34.7 %copy-start.10 = (bf16[1,256,768]{2,1,0:T(8,128)(2,1)S(1)}, bf16[1,256,768]{2,1,0:T(8,128)(2,1)}, u32[]{:S(2)}) copy-start(bf16[1,256,768]{2,1,0:T(8,128)(2,1)} %param.44) | copy-start | bytes 1179652
  123.9 34.7 %copy-start.49 = (f32[256]{0:T(256)S(1)}, f32[256]{0:T(256)}, u32[]{:S(2)}) copy-start(f32[256]{0:T(256)} %copy-done.48) | copy-start | bytes 3076
  123.9 34.7 %copy-start.53 = (f32[256]{0:T(256)S(1)}, f32[256]{0:T(256)}, u32[]{:S(2)}) copy-start(f32[256]{0:T(256)} %copy-done.52) | copy-start | bytes 3076
  123.9 34.8 %copy-start.58 = (f32[768]{0:T(1024)S(1)}, f32[768]{0:T(1024)}, u32[]{:S(2)}) copy-start(f32[768]{0:T(1024)} %param.42) | copy-start | bytes 9220
  124.0 95.0 %reduce-scatter.9.cloned.1.call-start = ((), (), s32[]{:S(2)}) async-start(), calls=%async_computation.9 | async-start | bytes 983040 | tf_op jit(solution)/shard_map/reduce_scatter | solution.py:274
  158.6 4.3 copy-start.25
  158.7 4.3 copy-start.26
  158.7 4.3 copy-start.50
  158.7 4.3 copy-start.54
  158.7 5.5 copy-start.14
  163.0 4.0 copy-start.9
  164.2 82.0 %copy-start.6 = (f32[256,768]{1,0:T(8,128)}, f32[256,768]{1,0:T(8,128)S(1)}, u32[]{:S(2)}) copy-start(f32[256,768]{1,0:T(8,128)S(1)} %fusion.39) | copy-start | bytes 2359300
  189.3 5.5 copy-start.3
  195.5 24.5 %copy-start.36 = (f32[256,32]{0,1:T(8,128)S(1)}, f32[256,32]{0,1:T(8,128)}, u32[]{:S(2)}) copy-start(f32[256,32]{0,1:T(8,128)} %copy-done.35) | copy-start | bytes 98308
  195.5 24.5 %copy-start.38 = (f32[256,32]{0,1:T(8,128)S(1)}, f32[256,32]{0,1:T(8,128)}, u32[]{:S(2)}) copy-start(f32[256,32]{0,1:T(8,128)} %get-tuple-element.483) | copy-start | bytes 98308
  195.5 24.7 %copy-start.15 = (bf16[768,384]{1,0:T(8,128)(2,1)S(1)}, bf16[768,384]{1,0:T(8,128)(2,1)}, u32[]{:S(2)}) copy-start(bf16[768,384]{1,0:T(8,128)(2,1)} %param.33) | copy-start | bytes 1769476
  195.6 48.2 %reduce-scatter.11.cloned.1.call-start = ((), (), s32[]{:S(2)}) async-start(), calls=%async_computation.10 | async-start | bytes 983040 | tf_op jit(solution)/shard_map/reduce_scatter | solution.py:277
  196.4 75.1 %all-reduce.8.cloned.1.call-start = ((), (), s32[]{:S(2)}) async-start(), calls=%async_computation.11 | async-start | bytes 786432 | tf_op jit(solution)/shard_map/psum | solution.py:308
  222.4 23.8 %copy-start.19 = (bf16[256,6,64]{0,2,1:T(8,128)(2,1)S(1)}, bf16[256,6,64]{0,2,1:T(8,128)(2,1)}, u32[]{:S(2)}) copy-start(bf16[256,6,64]{0,2,1:T(8,128)(2,1)} %copy-done.18) | copy-start | bytes 589828
  246.1 94.0 %reduce-scatter.19.cloned.1.call-start = ((), (), s32[]{:S(2)}) async-start(), calls=%async_computation.15 | async-start | bytes 1253376 | tf_op jit(solution)/shard_map/reduce_scatter | solution.py:314
  247.7 147.9 %reduce-scatter.15.cloned.1.call-start = ((), (), s32[]{:S(2)}) async-start(), calls=%async_computation.13 | async-start | bytes 1253376 | tf_op jit(solution)/shard_map/reduce_scatter | solution.py:312
  249.4 208.1 %reduce-scatter.13.cloned.1.call-start = ((), (), s32[]{:S(2)}) async-start(), calls=%async_computation.12 | async-start | bytes 1253376 | tf_op jit(solution)/shard_map/reduce_scatter | solution.py:311
  251.1 268.1 %reduce-scatter.17.cloned.1.call-start = ((), (), s32[]{:S(2)}) async-start(), calls=%async_computation.14 | async-start | bytes 1253376 | tf_op jit(solution)/shard_map/reduce_scatter | solution.py:313
  252.8 345.8 %reduce-scatter.21.cloned.1.call-start = ((), (), s32[]{:S(2)}) async-start(), calls=%async_computation.16 | async-start | bytes 5013504 | tf_op jit(solution)/shard_map/reduce_scatter | solution.py:315
  256.0 421.7 %reduce-scatter.23.cloned.1.call-start = ((), (), s32[]{:S(2)}) async-start(), calls=%async_computation.17 | async-start | bytes 5013504 | tf_op jit(solution)/shard_map/reduce_scatter | solution.py:316
  263.8 7.7 %copy-start.47 = (f32[256]{0:T(256)S(1)}, f32[256]{0:T(256)}, u32[]{:S(2)}) copy-start(f32[256]{0:T(256)} %copy-done.45) | copy-start | bytes 3076
  263.8 9.8 %copy-start.56 = (f32[768]{0:T(1024)S(1)}, f32[768]{0:T(1024)}, u32[]{:S(2)}) copy-start(f32[768]{0:T(1024)} %get-tuple-element.459) | copy-start | bytes 9220
  263.8 74.3 %copy-start.7 = (f32[256,768]{1,0:T(8,128)S(1)}, f32[256,768]{1,0:T(8,128)}, u32[]{:S(2)}) copy-start(f32[256,768]{1,0:T(8,128)} %copy-done.6) | copy-start | bytes 2359300
  263.8 413.9 %copy-start.1 = (bf16[1536,768]{1,0:T(8,128)(2,1)S(1)}, bf16[1536,768]{1,0:T(8,128)(2,1)}, u32[]{:S(2)}) copy-start(bf16[1536,768]{1,0:T(8,128)(2,1)} %param.41) | copy-start | bytes 7077892
  (26 other events, 41.3 us)
Sparse Core Ops, SparseCore 0:
  85.7 25.7 all-reduce.5
  124.1 34.5 all-reduce.9
  195.7 23.2 reduce-scatter.8
  221.2 22.5 reduce-scatter.10
  246.5 24.9 all-reduce.7
  276.0 58.0 reduce-scatter.18
  338.7 56.8 reduce-scatter.14
  400.3 57.1 reduce-scatter.12
  462.1 57.0 reduce-scatter.16
  524.0 74.5 reduce-scatter.20
  603.0 74.5 reduce-scatter.22
where the time goes:
time: 685 us; the launch traced here: 684 us
  waiting for transfers between devices  437 us (64%)
  blocking collectives  101 us (15%)
  matrix products  66.3 us (10%)
  other arithmetic  45.6 us (7%)
  local copies, waits for them, and re-layouts  17.4 us (3%)
  between operations  15.9 us (2%)
    reduce_scatter x1, waiting for transfers between devices, per_device(): lax.psum_scatter(grad_upw, ('seq', 'batch'), scatter_dimension=0, tiled=T...  79.4 us
    reduce_scatter x1, waiting for transfers between devices, per_device(): lax.psum_scatter(grad_down, ('seq', 'batch'), scatter_dimension=1, tiled=...  79.1 us
    psum x1, blocking collectives, per_device(): lax.psum((jnp.sum(grad_normed_first * unit_first, axis=0), jnp.sum(grad_n...  62.1 us
    reduce_scatter x1, waiting for transfers between devices, per_device(): lax.psum_scatter(grad_queryw, ('seq', 'batch'), scatter_dimension=0, tile...  61.9 us
    reduce_scatter x1, waiting for transfers between devices, per_device(): lax.psum_scatter(grad_valuew, ('seq', 'batch'), scatter_dimension=0, tile...  61.7 us
    reduce_scatter x1, waiting for transfers between devices, per_device(): lax.psum_scatter(grad_keyw, ('seq', 'batch'), scatter_dimension=0, tiled=...  55.5 us
    psum x1, waiting for transfers between devices, per_device(): lax.psum(jnp.dot(active, down_weight, preferred_element_type=jnp.float32)...  31.8 us
    all_gather x1, blocking collectives, per_device(): lax.all_gather(keys, 'seq', axis=0, tiled=True)  21.7 us
  transfers between devices with their start and end apart: 11, of which 10 were waited for; matrix products, arithmetic and copies ran while one was open for 5% of the time, Pallas kernels for 0%

commit v1 on v0

--- a/solution.py
+++ b/solution.py
@@ -1,3 +1,4 @@
+import functools
 import jax
 import jax.numpy as jnp
 from jax import lax
@@ -5,6 +6,14 @@
 
 HEAD_DIM = 64
 epsilon = 1e-05
+
+
+def wrap_the_copies(t0, axis_id):
+    tile_out = jnp.sum(lax.all_gather(t0, axis_name=axis_id), axis=0)
+    return tile_out
+
+
+trace_teams = functools.partial(wrap_the_copies, axis_id="tensor")
 
 
 def layer_parts(values, gain, shift):
@@ -155,9 +164,8 @@
 
     running = lax.fori_loop(0, count, output_step, jnp.zeros(split, jnp.float32))
     mixed = running.reshape(rows, local_width).astype(jnp.bfloat16)
-    attn_out = lax.psum(
-        jnp.dot(mixed, out_weight, preferred_element_type=jnp.float32).astype(jnp.bfloat16),
-        "tensor",
+    attn_out = trace_teams(
+        jnp.dot(mixed, out_weight, preferred_element_type=jnp.float32).astype(jnp.bfloat16)
     ).astype(jnp.float32)
     hidden = residual + attn_out
     normed_second, unit_second, scale_second = layer_parts(hidden, second_gain, second_shift)

time: 685 us -> 665 us (0.971)
  waiting for transfers between devices: 437 us -> 414 us
  blocking collectives: 101 us -> 110 us
    psum x1 -> x0, waiting for transfers between devices: 21.2 us -> none  [per_device(): lax.psum(jnp.dot(mixed, out_weight, preferred_element_type=jnp.float32).a...]
    all_gather x0 -> x1, blocking collectives: none -> 8.74 us  [wrap_the_copies(): tile_out = jnp.sum(lax.all_gather(t0, axis_name=axis_id), axis=0)]
  transfers between devices with their start and end apart: 11 -> 10, of which waited for: 10 -> 9; matrix products, arithmetic and copies ran while one was open for 5% -> 5% of each run, Pallas kernels for 0% -> 0%
where the time goes in v1:
time: 665 us; the launch traced here: 663 us
  waiting for transfers between devices  414 us (62%)
  blocking collectives  110 us (17%)
  matrix products  64 us (10%)
  other arithmetic  43 us (6%)
  between operations  16.2 us (2%)
  local copies, waits for them, and re-layouts  15.8 us (2%)
    reduce_scatter x1, waiting for transfers between devices, per_device(): lax.psum_scatter(grad_down, ('seq', 'batch'), scatter_dimension=1, tiled=...  79.4 us
    reduce_scatter x1, waiting for transfers between devices, per_device(): lax.psum_scatter(grad_upw, ('seq', 'batch'), scatter_dimension=0, tiled=T...  79 us
    psum x1, blocking collectives, per_device(): lax.psum((jnp.sum(grad_normed_first * unit_first, axis=0), jnp.sum(grad_n...  61.8 us
    reduce_scatter x1, waiting for transfers between devices, per_device(): lax.psum_scatter(grad_valuew, ('seq', 'batch'), scatter_dimension=0, tile...  61.3 us
    reduce_scatter x1, waiting for transfers between devices, per_device(): lax.psum_scatter(grad_queryw, ('seq', 'batch'), scatter_dimension=0, tile...  61.3 us
    reduce_scatter x1, waiting for transfers between devices, per_device(): lax.psum_scatter(grad_keyw, ('seq', 'batch'), scatter_dimension=0, tiled=...  54.8 us
    psum x1, waiting for transfers between devices, per_device(): lax.psum(jnp.dot(active, down_weight, preferred_element_type=jnp.float32)...  32 us
    all_gather x1, blocking collectives, per_device(): lax.all_gather(keys, 'seq', axis=0, tiled=True)  21.7 us
  transfers between devices with their start and end apart: 10, of which 9 were waited for; matrix products, arithmetic and copies ran while one was open for 5% of the time, Pallas kernels for 0%

profile of v1, /device:TPU:0, one launch (start us, length us, event | category | flops | bytes accessed | tf_op | source)
XLA Modules:
  0.0 663.4 jit_solution(17510489261005983989)
XLA Ops:
  9.9 2.1 copy.54
  13.2 2.3 fusion.53
  15.5 2.3 fusion.55
  19.9 2.1 multiply_subtract_fusion.2
  22.0 21.7 %all_gather.14 = bf16[1024,384]{0,1:T(8,128)(2,1)} all-gather(bf16[256,384]{0,1:T(8,128)(2,1)S(1)} %bitcast.213), channel_id=1, replica_groups=mesh['seq'=4,'batch'=4,'tensor'=2] {'seq'}, dimensions={0}, use_global_device_ids=true | all-gather | bytes 983040 | tf_op jit(solution)/shard_map/all_gather | solution.py:112
  43.7 2.6 fusion.67
  46.7 1.6 fusion.82
  49.5 17.3 %all_gather.15 = bf16[1024,384]{1,0:T(8,128)(2,1)S(1)} all-gather(bf16[256,384]{1,0:T(8,128)(2,1)S(1)} %convolution_convert_fusion.4), channel_id=1, replica_groups=mesh['seq'=4,'batch'=4,'tensor'=2] {'seq'}, dimensions={0}, use_global_device_ids=true | all-gather | bytes 983040 | tf_op jit(solution)/shard_map/all_gather | solution.py:113
  68.2 6.7 %conditional.4 = (f32[6,256]{1,0:T(8,128)}, f32[6,256]{1,0:T(8,128)}) conditional(s32[]{:T(128)} %convert_element_type.200, (f32[6,256]{1,0:T(8,128)}, f32[6,256]{1,0:T(8,128)S(1)}) %tuple.66, (pred[256,1024]{1,0:T(8,128)(4,1)S(1)}, bf16[1024,384]{0,1:T(8,128)(2,1)S(1)}, bf16[256,6,64]{0,2,1:T(8,128)(2,1)}, f32[6,256]{1,0:T(8,128)}, ...), branch_computations={%region_7.8_spmd, %region_8.11_spmd} | conditional | flops 210766848 | bytes 14170128 | solution.py:139
  68.2 2.1 select_reduce_fusion.1
  71.0 1.9 select_reduce_fusion
  75.7 5.3 conditional.5
  76.8 4.1 fusion.4
  82.5 8.7 %all-gather = bf16[512,768]{1,0:T(8,128)(2,1)} all-gather(bf16[256,768]{1,0:T(8,128)(2,1)S(1)} %convolution_convert_fusion.2), channel_id=2, replica_groups=mesh['seq'=4,'batch'=4,'tensor'=2] {'tensor'}, dimensions={0}, use_global_device_ids=true | all-gather | bytes 1179648 | tf_op jit(solution)/shard_map/all_gather | solution.py:12
  93.7 2.5 convolution_add_fusion
  96.3 1.8 convolution_convert_fusion.1
  99.5 2.4 convert_reduce_fusion
  104.4 2.7 multiply_reduce_fusion.2
  107.1 32.0 %all-reduce.7.cloned.1.call-done = (bf16[256,768]{1,0:T(8,128)(2,1)}, bf16[256,768]{1,0:T(8,128)(2,1)}) async-done(((bf16[256,768]{1,0:T(8,128)(2,1)}, bf16[256,768]{1,0:T(8,128)(2,1)}), (bf16[256,768]{1,0:T(8,128)(2,1)}, bf16[256,768]{1,0:T(8,128)(2,1)})) %all-reduce.7.cloned.1.call-update) | async-done | bytes 786448 | tf_op jit(solution)/shard_map/psum | solution.py:177
  139.1 4.3 multiply_reduce_fusion.4
  145.7 1.7 copy.56
  147.5 11.1 %conditional.6 = (f32[6,256]{1,0:T(8,128)S(1)}) conditional(s32[]{:T(128)} %convert_element_type.200, f32[6,256]{1,0:T(8,128)S(1)} %broadcast.362, (pred[256,1024]{1,0:T(8,128)(4,1)}, bf16[1024,384]{0,1:T(8,128)(2,1)S(1)}, bf16[256,6,64]{0,2,1:T(8,128)(2,1)}, f32[6,256]{1,0:T(8,128)}, f32[6,256]{1,0:T(8,128)}, ...), branch_computations={%region_20.21_spmd, %region_21.23_spmd} | conditional | flops 410517504 | bytes 16420872 | solution.py:239
  147.5 4.6 fusion.84
  153.2 5.3 multiply_reduce_fusion
  158.6 16.6 %conditional.7 = (f32[256,6,64]{0,2,1:T(8,128)}, bf16[1024,384]{0,1:T(8,128)(2,1)S(1)}, bf16[1024,384]{0,1:T(8,128)(2,1)S(1)}) conditional(s32[]{:T(128)} %convert_element_type.200, f32[256,6,64]{0,2,1:T(8,128)} %broadcast.358, (pred[256,1024]{1,0:T(8,128)(4,1)}, bf16[1024,384]{0,1:T(8,128)(2,1)S(1)}, bf16[256,6,64]{0,2,1:T(8,128)(2,1)}, ...), branch_computations={%region_23.24_spmd, %region_24.25_spmd} | conditional | flops 1017741312 | bytes 61622352 | solution.py:273
  158.8 5.5 select_divide_fusion
  165.5 4.2 multiply_convert_fusion
  169.8 1.7 fusion.85
  171.5 3.0 fusion.8
  178.0 21.6 %reduce-scatter.9.cloned.1.call-done = bf16[256,384]{0,1:T(8,128)(2,1)} async-done(((bf16[1024,384]{0,1:T(8,128)(2,1)}), bf16[256,384]{0,1:T(8,128)(2,1)}) %reduce-scatter.9.cloned.1.call-update) | async-done | bytes 196624 | tf_op jit(solution)/shard_map/reduce_scatter | solution.py:282
  203.7 20.9 %reduce-scatter.11.cloned.1.call-done = bf16[256,384]{0,1:T(8,128)(2,1)} async-done(((bf16[1024,384]{0,1:T(8,128)(2,1)}), bf16[256,384]{0,1:T(8,128)(2,1)}) %reduce-scatter.11.cloned.1.call-update) | async-done | bytes 196624 | tf_op jit(solution)/shard_map/reduce_scatter | solution.py:285
  224.6 2.3 fusion.15
  228.6 1.6 fusion.57
  230.3 1.6 fusion.59
  232.0 1.6 fusion.72
  233.7 3.1 fusion.64
  238.3 3.1 fusion.75
  242.1 2.5 multiply_convert_fusion.1
  246.9 2.5 pad_maximum_fusion.2
  249.4 3.1 all-reduce.5.cloned.1.call-done
  252.5 2.0 fusion.46
  254.5 61.8 %all-reduce = (f32[768]{0:T(1024)}, f32[768]{0:T(1024)}, f32[768]{0:T(1024)}, f32[768]{0:T(1024)}, f32[1536]{0:T(1024)}, /*index=5*/f32[768]{0:T(1024)}, f32[9]{0:T(128)}, f32[3]{0:T(128)}) all-reduce(f32[768]{0:T(1024)} %get-tuple-element.439, ...), channel_id=1, replica_groups=mesh['seq'=4,'batch'=4,'tensor'=2] {'seq','batch'}, use_global_device_ids=true, to_apply=%region_31.32 | all-reduce | flops 5388 | bytes 43104 | tf_op jit(solution)/shard_map/psum | solution.py:333
  318.7 2.1 fusion.51
  320.8 54.8 %reduce-scatter.15.cloned.1.call-done = f32[48,384]{1,0:T(8,128)} async-done(((f32[768,384]{1,0:T(8,128)}), f32[48,384]{1,0:T(8,128)}) %reduce-scatter.15.cloned.1.call-update) | async-done | bytes 73744 | tf_op jit(solution)/shard_map/reduce_scatter | solution.py:320
  375.7 61.3 %reduce-scatter.13.cloned.1.call-done = f32[48,384]{1,0:T(8,128)} async-done(((f32[768,384]{1,0:T(8,128)}), f32[48,384]{1,0:T(8,128)}) %reduce-scatter.13.cloned.1.call-update) | async-done | bytes 73744 | tf_op jit(solution)/shard_map/reduce_scatter | solution.py:319
  436.9 61.3 %reduce-scatter.17.cloned.1.call-done = f32[48,384]{1,0:T(8,128)} async-done(((f32[768,384]{1,0:T(8,128)}), f32[48,384]{1,0:T(8,128)}) %reduce-scatter.17.cloned.1.call-update) | async-done | bytes 73744 | tf_op jit(solution)/shard_map/reduce_scatter | solution.py:321
  498.2 79.0 %reduce-scatter.21.cloned.1.call-done = f32[48,1536]{1,0:T(8,128)} async-done(((f32[768,1536]{1,0:T(8,128)}), f32[48,1536]{1,0:T(8,128)}) %reduce-scatter.21.cloned.1.call-update) | async-done | bytes 294928 | tf_op jit(solution)/shard_map/reduce_scatter | solution.py:323
  577.2 79.4 %reduce-scatter.23.cloned.1.call-done = f32[1536,48]{0,1:T(8,128)} async-done(((f32[1536,768]{0,1:T(8,128)}), f32[1536,48]{0,1:T(8,128)}) %reduce-scatter.23.cloned.1.call-update) | async-done | bytes 294928 | tf_op jit(solution)/shard_map/reduce_scatter | solution.py:324
  (210 shorter events, 40.6 us)
Async XLA Ops:
  7.2 89.0 %copy-start = (bf16[1536,768]{1,0:T(8,128)(2,1)S(1)}, bf16[1536,768]{1,0:T(8,128)(2,1)}, u32[]{:S(2)}) copy-start(bf16[1536,768]{1,0:T(8,128)(2,1)} %param.41) | copy-start | bytes 7077892
  7.2 6.0 copy-start.2
  7.2 4.8 copy-start.19
  7.2 5.9 copy-start.40
  7.2 5.9 copy-start.45
  7.3 131.8 %all-reduce.7.cloned.1.call-start = ((), (), s32[]{:S(2)}) async-start(), calls=%async_computation.17 | async-start | bytes 1572864 | tf_op jit(solution)/shard_map/psum | solution.py:177
  8.7 40.3 %copy-start.43 = (f32[256]{0:T(256)}, f32[256]{0:T(256)S(1)}, u32[]{:S(2)}) copy-start(f32[256]{0:T(256)S(1)} %broadcast_multiply_fusion.6) | copy-start | bytes 3076
  9.9 39.0 %copy-start.47 = (f32[256]{0:T(256)}, f32[256]{0:T(256)S(1)}, u32[]{:S(2)}) copy-start(f32[256]{0:T(256)S(1)} %add_rsqrt_fusion.1) | copy-start | bytes 3076
  12.1 5.7 copy-start.59
  15.5 30.9 %copy-start.66 = (s32[1,3]{1,0:T(1,128)S(1)}, s32[1,3]{1,0:T(1,128)}, u32[]{:S(2)}) copy-start(s32[1,3]{1,0:T(1,128)} %param.29) | copy-start | bytes 40
  15.5 33.5 %copy-start.37 = (bf16[768,384]{1,0:T(8,128)(2,1)S(1)}, bf16[768,384]{1,0:T(8,128)(2,1)}, u32[]{:S(2)}) copy-start(bf16[768,384]{1,0:T(8,128)(2,1)} %param.35) | copy-start | bytes 1769476
  19.9 23.8 %copy-start.38 = (f32[256,32]{0,1:T(8,128)}, f32[256,32]{0,1:T(8,128)S(1)}, u32[]{:S(2)}) copy-start(f32[256,32]{0,1:T(8,128)S(1)} %get-tuple-element.485) | copy-start | bytes 98308
  49.0 17.8 %copy-start.34 = (f32[256,6,32]{0,2,1:T(8,128)S(1)}, f32[256,6,32]{0,2,1:T(8,128)}, u32[]{:S(2)}) copy-start(f32[256,6,32]{0,2,1:T(8,128)} %get-tuple-element.473) | copy-start | bytes 589828
  49.0 17.8 %copy-start.35 = (f32[256,6,32]{0,2,1:T(8,128)S(1)}, f32[256,6,32]{0,2,1:T(8,128)}, u32[]{:S(2)}) copy-start(f32[256,6,32]{0,2,1:T(8,128)} %get-tuple-element.474) | copy-start | bytes 589828
  49.0 19.2 %copy-start.9 = (bf16[1024,384]{0,1:T(8,128)(2,1)S(1)}, bf16[1024,384]{0,1:T(8,128)(2,1)}, u32[]{:S(2)}) copy-start(bf16[1024,384]{0,1:T(8,128)(2,1)} %all_gather.14) | copy-start | bytes 2359300
  49.0 19.1 %copy-start.18 = (pred[256,1024]{1,0:T(8,128)(4,1)S(1)}, pred[256,1024]{1,0:T(8,128)(4,1)}, u32[]{:S(2)}) copy-start(pred[256,1024]{1,0:T(8,128)(4,1)} %get-tuple-element.464) | copy-start | bytes 786436
  66.8 8.8 %copy-start.4 = (bf16[1024,384]{1,0:T(8,128)(2,1)}, bf16[1024,384]{1,0:T(8,128)(2,1)S(1)}, u32[]{:S(2)}) copy-start(bf16[1024,384]{1,0:T(8,128)(2,1)S(1)} %all_gather.15) | copy-start | bytes 2359300
  80.9 10.3 %copy-start.20 = (bf16[256,6,64]{0,2,1:T(8,128)(2,1)}, bf16[256,6,64]{0,2,1:T(8,128)(2,1)S(1)}, u32[]{:S(2)}) copy-start(bf16[256,6,64]{0,2,1:T(8,128)(2,1)S(1)} %convert_element_type.208) | copy-start | bytes 589828
  80.9 12.1 %copy-start.61 = (f32[9]{0:T(128)S(1)}, f32[9]{0:T(128)}, u32[]{:S(2)}) copy-start(f32[9]{0:T(128)} %param.43) | copy-start | bytes 112
  81.0 12.7 %copy-start.39 = (f32[768]{0:T(1024)S(1)}, f32[768]{0:T(1024)}, u32[]{:S(2)}) copy-start(f32[768]{0:T(1024)} %param.37) | copy-start | bytes 9220
  81.0 12.7 %copy-start.41 = (f32[768]{0:T(1024)S(1)}, f32[768]{0:T(1024)}, u32[]{:S(2)}) copy-start(f32[768]{0:T(1024)} %param.38) | copy-start | bytes 9220
  81.0 12.7 %copy-start.65 = (f32[1536]{0:T(1024)S(1)}, f32[1536]{0:T(1024)}, u32[]{:S(2)}) copy-start(f32[1536]{0:T(1024)} %param.40) | copy-start | bytes 18436
  104.3 34.7 %copy-start.51 = (f32[256]{0:T(256)S(1)}, f32[256]{0:T(256)}, u32[]{:S(2)}) copy-start(f32[256]{0:T(256)} %copy-done.50) | copy-start | bytes 3076
  104.3 34.7 %copy-start.55 = (f32[256]{0:T(256)S(1)}, f32[256]{0:T(256)}, u32[]{:S(2)}) copy-start(f32[256]{0:T(256)} %copy-done.54) | copy-start | bytes 3076
  104.3 34.7 %copy-start.60 = (f32[768]{0:T(1024)S(1)}, f32[768]{0:T(1024)}, u32[]{:S(2)}) copy-start(f32[768]{0:T(1024)} %param.42) | copy-start | bytes 9220
  104.4 95.2 %reduce-scatter.9.cloned.1.call-start = ((), (), s32[]{:S(2)}) async-start(), calls=%async_computation.8 | async-start | bytes 983040 | tf_op jit(solution)/shard_map/reduce_scatter | solution.py:282
  139.1 4.3 copy-start.28
  139.1 4.3 copy-start.29
  139.1 4.3 copy-start.52
  139.1 4.3 copy-start.56
  139.1 5.5 copy-start.16
  143.4 4.1 copy-start.5
  144.6 82.4 %copy-start.7 = (f32[256,768]{1,0:T(8,128)}, f32[256,768]{1,0:T(8,128)S(1)}, u32[]{:S(2)}) copy-start(f32[256,768]{1,0:T(8,128)S(1)} %fusion.39) | copy-start | bytes 2359300
  169.8 4.7 copy-start.3
  176.1 48.5 %reduce-scatter.11.cloned.1.call-start = ((), (), s32[]{:S(2)}) async-start(), calls=%async_computation.9 | async-start | bytes 983040 | tf_op jit(solution)/shard_map/reduce_scatter | solution.py:285
  176.9 24.7 %copy-start.17 = (bf16[768,384]{1,0:T(8,128)(2,1)S(1)}, bf16[768,384]{1,0:T(8,128)(2,1)}, u32[]{:S(2)}) copy-start(bf16[768,384]{1,0:T(8,128)(2,1)} %param.33) | copy-start | bytes 1769476
  176.9 75.6 %all-reduce.5.cloned.1.call-start = ((), (), s32[]{:S(2)}) async-start(), calls=%async_computation.10 | async-start | bytes 786432 | tf_op jit(solution)/shard_map/psum | solution.py:316
  203.7 23.3 %copy-start.21 = (bf16[256,6,64]{0,2,1:T(8,128)(2,1)S(1)}, bf16[256,6,64]{0,2,1:T(8,128)(2,1)}, u32[]{:S(2)}) copy-start(bf16[256,6,64]{0,2,1:T(8,128)(2,1)} %copy-done.20) | copy-start | bytes 589828
  227.0 93.8 %reduce-scatter.19.cloned.1.call-start = ((), (), s32[]{:S(2)}) async-start(), calls=%async_computation.14 | async-start | bytes 1253376 | tf_op jit(solution)/shard_map/reduce_scatter | solution.py:322
  228.5 147.1 %reduce-scatter.15.cloned.1.call-start = ((), (), s32[]{:S(2)}) async-start(), calls=%async_computation.12 | async-start | bytes 1253376 | tf_op jit(solution)/shard_map/reduce_scatter | solution.py:320
  230.3 206.7 %reduce-scatter.13.cloned.1.call-start = ((), (), s32[]{:S(2)}) async-start(), calls=%async_computation.11 | async-start | bytes 1253376 | tf_op jit(solution)/shard_map/reduce_scatter | solution.py:319
  231.9 266.3 %reduce-scatter.17.cloned.1.call-start = ((), (), s32[]{:S(2)}) async-start(), calls=%async_computation.13 | async-start | bytes 1253376 | tf_op jit(solution)/shard_map/reduce_scatter | solution.py:321
  233.6 343.6 %reduce-scatter.21.cloned.1.call-start = ((), (), s32[]{:S(2)}) async-start(), calls=%async_computation.15 | async-start | bytes 5013504 | tf_op jit(solution)/shard_map/reduce_scatter | solution.py:323
  236.8 419.8 %reduce-scatter.23.cloned.1.call-start = ((), (), s32[]{:S(2)}) async-start(), calls=%async_computation.16 | async-start | bytes 5013504 | tf_op jit(solution)/shard_map/reduce_scatter | solution.py:324
  244.6 7.9 %copy-start.49 = (f32[256]{0:T(256)S(1)}, f32[256]{0:T(256)}, u32[]{:S(2)}) copy-start(f32[256]{0:T(256)} %copy-done.47) | copy-start | bytes 3076
  244.6 9.9 %copy-start.58 = (f32[768]{0:T(1024)S(1)}, f32[768]{0:T(1024)}, u32[]{:S(2)}) copy-start(f32[768]{0:T(1024)} %get-tuple-element.459) | copy-start | bytes 9220
  244.6 74.1 %copy-start.8 = (f32[256,768]{1,0:T(8,128)S(1)}, f32[256,768]{1,0:T(8,128)}, u32[]{:S(2)}) copy-start(f32[256,768]{1,0:T(8,128)} %copy-done.7) | copy-start | bytes 2359300
  244.6 412.0 %copy-start.1 = (bf16[1536,768]{1,0:T(8,128)(2,1)S(1)}, bf16[1536,768]{1,0:T(8,128)(2,1)}, u32[]{:S(2)}) copy-start(bf16[1536,768]{1,0:T(8,128)(2,1)} %param.41) | copy-start | bytes 7077892
  (29 other events, 51.3 us)
Sparse Core Ops, SparseCore 0:
  104.5 34.5 all-reduce.6
  176.2 23.3 reduce-scatter.8
  202.0 22.5 reduce-scatter.10
  227.4 24.9 all-reduce.4
  256.5 57.8 reduce-scatter.18
  318.5 57.1 reduce-scatter.14
  379.8 57.0 reduce-scatter.12
  441.1 57.0 reduce-scatter.16
  502.6 74.5 reduce-scatter.20
  582.0 74.5 reduce-scatter.22
